TPU v7x, 32 devices: a whole 2x2x4 slice. The times are simulated.
32 devices in a mesh: section: 4 (over x, core), mp: 8 (over z, y).
Axes of the slice: x: 2, y: 2, z: 4, core: 2. Of those that a mesh axis runs over, the one named last changes fastest.
Arguments:
- activations: bfloat16 [4, 64, 4096], P('section', 'mp'), may hold values from -24 to 24
- enc_weight: bfloat16 [4, 4096, 4096], P('section', None, 'mp'), may hold values from -0.046875 to 0.046875
- enc_bias: float32 [4096], P('mp'), may hold values from -4 to 4
- dec_weight: bfloat16 [4096, 4, 4096], P('mp', 'section'), may hold values from -2.1875 to 2.1875
- dec_bias: float32 [4, 4096], P('section'), may hold values from -3 to 3
Outputs:
- loss: float32 [], replicated
- grad_dec: bfloat16 [4096, 4, 4096], P('mp', 'section')
- grad_bias: float32 [4, 4096], P('section', 'mp')
All inputs are finite; a program needn't handle non-finite values.
Results may differ from a plain program's by a relative error of at most 0.009.
Values may be sent and summed in bfloat16 or wider, within the bound.
A program may use at most 64 MiB of HBM per device.

v0:
```python
import jax
import jax.numpy as jnp
from jax import lax
from jax.sharding import PartitionSpec as P

penalty_weight = 2.0


def local(activations, enc_weight, enc_bias, dec_weight, dec_bias):
    all_rows = lax.all_gather(activations[0], "mp", axis=0, tiled=True)
    token_count = all_rows.shape[0]
    partial_value = jnp.dot(all_rows, enc_weight[0], preferred_element_type=jnp.float32)
    w_dec = dec_weight[:, 0, :]
    layer_norm = jnp.sqrt(jnp.sum(jnp.square(w_dec.astype(jnp.float32)), axis=1) + 1e-06)
    pre_sum, norm_total = (
        lax.psum(partial_value.astype(jnp.bfloat16), "section").astype(jnp.float32),
        lax.psum(layer_norm.astype(jnp.bfloat16), "section").astype(jnp.float32),
    )
    latents = jnp.maximum(pre_sum + enc_bias[None, :], 0.0).astype(jnp.bfloat16)
    latent_float = latents.astype(jnp.float32)
    latent_sum = jnp.sum(latent_float, axis=0)
    penalty_part = penalty_weight / token_count * jnp.sum(latent_float * norm_total[None, :])
    penalty_part = jnp.where(lax.axis_index("section") == 0, penalty_part, 0.0)
    coef = penalty_weight * latent_sum / token_count / layer_norm
    col_width = w_dec.shape[1] // lax.axis_size("mp")
    first_col = lax.axis_index("mp") * col_width
    recon_t = lax.psum_scatter(
        lax.dot_general(
            w_dec, latents, (((0,), (1,)), ((), ())), preferred_element_type=jnp.float32
        ),
        "mp",
        scatter_dimension=0,
        tiled=True,
    )
    bias_cols = lax.dynamic_slice_in_dim(dec_bias[0], first_col, col_width, 0)
    x_cols = lax.dynamic_slice_in_dim(all_rows, first_col, col_width, 1)
    error_cols = recon_t + bias_cols[:, None] - x_cols.T.astype(jnp.float32)
    square_sum = jnp.sum(error_cols * error_cols)
    scaled = 2.0 * error_cols / token_count
    grad_rec_t = scaled.astype(jnp.bfloat16)
    grad_bias = jnp.sum(scaled, axis=1)[None, :]
    grad_sum = lax.dot_general(
        latents,
        lax.all_gather(grad_rec_t, "mp", axis=0, tiled=True),
        (((0,), (1,)), ((), ())),
        preferred_element_type=jnp.float32,
    )
    grad_dec = (grad_sum + coef[:, None] * w_dec.astype(jnp.float32)).astype(jnp.bfloat16)[
        :, None, :
    ]
    loss = lax.psum(square_sum / token_count + penalty_part, ("section", "mp"))
    return (loss, grad_dec, grad_bias)


def solution(mesh):
    in_specs = (
        P("section", "mp", None),
        P("section", None, "mp"),
        P("mp"),
        P("mp", "section", None),
        P("section", None),
    )
    out_specs = (P(), P("mp", "section", None), P("section", "mp"))
    return jax.shard_map(local, mesh=mesh, in_specs=in_specs, out_specs=out_specs, check_vma=False)
```

profile of v0, /device:TPU:0, one launch (start us, length us, event | category | flops | bytes accessed | tf_op | source)
XLA Modules:
  0.0 231.0 jit_solution(3103381486748929811)
XLA Ops:
  7.2 0.0 copy-start
  7.2 0.0 copy-start.2
  7.2 0.0 all-reduce.2.cloned.1.call-start
  7.2 33.2 %all-gather = bf16[1,64,4096]{2,1,0:T(8,128)(2,1)S(1)} all-gather(bf16[1,8,4096]{2,1,0:T(8,128)(2,1)} %param.5), channel_id=2, replica_groups=mesh['section'=4,'mp'=8] {'mp'}, dimensions={1}, use_global_device_ids=true | all-gather | bytes 589824 | tf_op jit(solution)/shard_map/all_gather | solution.py:10
  40.5 3.7 %fusion.7 = bf16[64,512]{1,0:T(8,128)(2,1)} fusion(bf16[1,4096,512]{2,1,0:T(8,128)(2,1)} %param.6, bf16[1,64,4096]{2,1,0:T(8,128)(2,1)S(1)} %all-gather), kind=kOutput, calls=%fused_computation.10 | convolution fusion | flops 268468224 | bytes 4784128 | tf_op jit(solution)/shard_map/dot_general | solution.py:12
  44.1 0.0 all-reduce.2.cloned.1.call-update
  44.2 0.0 reduce-scatter.2.cloned.1.call-start
  44.2 32.7 %all-reduce.2.cloned.1.call-done = bf16[64,512]{1,0:T(8,128)(2,1)} async-done(((bf16[64,512]{1,0:T(8,128)(2,1)}), bf16[64,512]{1,0:T(8,128)(2,1)}) %all-reduce.2.cloned.1.call-update) | async-done | bytes 65552 | tf_op jit(solution)/shard_map/psum | solution.py:16
  76.9 0.0 copy-done.2
  76.9 0.0 copy-start.1
  76.9 4.1 %convolution_bitcast_fusion = f32[4096,64]{0,1:T(8,128)} fusion(bf16[512,1,4096]{2,0,1:T(8,128)(2,1)} %param.8, bf16[64,512]{1,0:T(8,128)(2,1)} %all-reduce.2.cloned.1.call-done, f32[512]{0:T(512)S(1)} %copy-done.2), kind=kOutput, calls=%fused_computation.6 | convolution fusion | flops 268566528 | bytes 5310464 | tf_op jit(solution)/shard_map/dot_general | solution.py:28
  81.0 0.0 reduce-scatter.2.cloned.1.call-update
  81.1 3.1 %fusion = f32[512]{0:T(512)S(1)} fusion(bf16[512,1,4096]{2,0,1:T(8,128)(2,1)} %param.8), kind=kLoop, calls=%fused_computation.2 | loop fusion | flops 6290944 | bytes 4196352 | tf_op jit(solution)/shard_map/reduce_sum | solution.py:14
  84.1 5.8 %psum.22 = bf16[512]{0:T(512)(128)(2,1)S(1)} all-reduce(bf16[512]{0:T(512)(128)(2,1)S(1)} %sqrt_convert_fusion), channel_id=1, replica_groups=mesh['section'=4,'mp'=8] {'section'}, use_global_device_ids=true, to_apply=%region_4.0 | all-reduce | flops 512 | bytes 2048 | tf_op jit(solution)/shard_map/psum | solution.py:17
  89.9 0.0 copy-done
  89.9 0.0 copy-done.1
  89.9 0.6 convert_reduce_fusion
  91.2 54.2 %reduce-scatter.2.cloned.1.call-done = f32[512,64]{0,1:T(8,128)} async-done(((f32[4096,64]{0,1:T(8,128)}), f32[512,64]{0,1:T(8,128)}) %reduce-scatter.2.cloned.1.call-update) | async-done | bytes 131088 | tf_op jit(solution)/shard_map/reduce_scatter | solution.py:27
  145.5 1.5 multiply_reduce_fusion.1
  147.7 39.8 %psum.23 = f32[]{:T(128)} all-reduce(f32[]{:T(128)S(6)} %add.54), channel_id=1, replica_groups=mesh['section'=4,'mp'=8] {'section','mp'}, use_global_device_ids=true, to_apply=%region_6.7 | all-reduce | flops 1 | bytes 8 | tf_op jit(solution)/shard_map/psum | solution.py:51
  187.5 31.2 %all_gather.7 = bf16[4096,64]{0,1:T(8,128)(2,1)S(1)} all-gather(bf16[512,64]{0,1:T(8,128)(2,1)S(1)} %get-tuple-element.7), channel_id=1, replica_groups=mesh['section'=4,'mp'=8] {'mp'}, dimensions={0}, use_global_device_ids=true | all-gather | bytes 589824 | tf_op jit(solution)/shard_map/all_gather | solution.py:44
  218.7 5.5 %fusion.3 = bf16[512,1,4096]{2,0,1:T(8,128)(2,1)} fusion(bf16[4096,64]{0,1:T(8,128)(2,1)S(1)} %all_gather.7, bf16[512,1,4096]{2,0,1:T(8,128)(2,1)} %param.8, f32[512]{0:T(512)S(1)} %rsqrt_multiply_fusion, bf16[64,512]{1,0:T(8,128)(2,1)S(1)} %copy-done.1, f32[512]{0:T(512)S(1)} %copy-done.2), kind=kOutput, calls=%fused_computation.5 | convolution fusion | flops 276955136 | bytes 8982528 | tf_op jit(solution)/shard_map/dot_general | solution.py:42
  (4 shorter events, 0.0 us)
Async XLA Ops:
  7.2 82.8 %copy-start = (f32[1,4096]{1,0:T(1,128)S(1)}, f32[1,4096]{1,0:T(1,128)}, u32[]{:S(2)}) copy-start(f32[1,4096]{1,0:T(1,128)} %param.9) | copy-start | bytes 49156
  7.2 69.8 %copy-start.2 = (f32[512]{0:T(512)S(1)}, f32[512]{0:T(512)}, u32[]{:S(2)}) copy-start(f32[512]{0:T(512)} %param.7) | copy-start | bytes 6148
  7.2 69.8 %all-reduce.2.cloned.1.call-start = ((), (), s32[]{:S(2)}) async-start(), calls=%async_computation.1 | async-start | bytes 131072 | tf_op jit(solution)/shard_map/psum | solution.py:16
  44.2 101.3 %reduce-scatter.2.cloned.1.call-start = ((), (), s32[]{:S(2)}) async-start(), calls=%async_computation.2 | async-start | bytes 1179648 | tf_op jit(solution)/shard_map/reduce_scatter | solution.py:27
  76.9 13.0 %copy-start.1 = (bf16[64,512]{1,0:T(8,128)(2,1)S(1)}, bf16[64,512]{1,0:T(8,128)(2,1)}, u32[]{:S(2)}) copy-start(bf16[64,512]{1,0:T(8,128)(2,1)} %all-reduce.2.cloned.1.call-done) | copy-start | bytes 196612
Sparse Core Ops, SparseCore 0:
  44.3 32.6 all-reduce.1
  81.2 64.2 reduce-scatter.1
where the time goes:
time: 231 us
  blocking collectives  110 us (48%)
  waiting for transfers between devices  87 us (38%)
  between operations  15.4 us (7%)
  matrix products  13.2 us (6%)
  other arithmetic  5.29 us (2%)
    reduce_scatter x1, waiting for transfers between devices, local(): lax.psum_scatter(lax.dot_general(w_dec, latents, (((0,), (1,)), ((), ()))...  54.2 us
    psum x1, blocking collectives, local(): loss = lax.psum(square_sum / token_count + penalty_part, ('section', 'mp'))  39.8 us
    all_gather x1, blocking collectives, local(): all_rows = lax.all_gather(activations[0], 'mp', axis=0, tiled=True)  33.2 us
    psum x1, waiting for transfers between devices, local(): lax.psum(partial_value.astype(jnp.bfloat16), 'section').astype(jnp.float32)  32.7 us
    all_gather x1, blocking collectives, local(): lax.all_gather(grad_rec_t, 'mp', axis=0, tiled=True)  31.2 us
    psum x1, blocking collectives, local(): lax.psum(layer_norm.astype(jnp.bfloat16), 'section').astype(jnp.float32)  5.77 us
    dot_general x1, matrix products, local(): lax.dot_general(latents, lax.all_gather(grad_rec_t, 'mp', axis=0, tiled=T...  5.49 us
  transfers between devices with their start and end apart: 2, of which 2 were waited for; matrix products, arithmetic and copies ran while one was open for 2% of the time, Pallas kernels for 0%

commit v1 on v0

--- a/solution.py
+++ b/solution.py
@@ -48,7 +48,8 @@
     grad_dec = (grad_sum + coef[:, None] * w_dec.astype(jnp.float32)).astype(jnp.bfloat16)[
         :, None, :
     ]
-    loss = lax.psum(square_sum / token_count + penalty_part, ("section", "mp"))
+    partial = lax.psum(square_sum / token_count + penalty_part, "mp")
+    loss = lax.psum(partial, "section")
     return (loss, grad_dec, grad_bias)
 
 

time: 231 us -> 218 us (0.944)
  blocking collectives: 110 us -> 96.6 us
    psum x1 -> x2, blocking collectives: 39.8 us -> 26.1 us  [the longest x1 19.8 us: local(): partial = lax.psum(square_sum / token_count + penalty_part, 'mp')]
where the time goes in v1:
time: 218 us
  blocking collectives  96.6 us (44%)
  waiting for transfers between devices  87 us (40%)
  between operations  15.4 us (7%)
  matrix products  13.2 us (6%)
  other arithmetic  5.29 us (2%)
    reduce_scatter x1, waiting for transfers between devices, local(): lax.psum_scatter(lax.dot_general(w_dec, latents, (((0,), (1,)), ((), ()))...  54.2 us
    all_gather x1, blocking collectives, local(): all_rows = lax.all_gather(activations[0], 'mp', axis=0, tiled=True)  33.2 us
    psum x1, waiting for transfers between devices, local(): lax.psum(partial_value.astype(jnp.bfloat16), 'section').astype(jnp.float32)  32.7 us
    all_gather x1, blocking collectives, local(): lax.all_gather(grad_rec_t, 'mp', axis=0, tiled=True)  31.5 us
    psum x1, blocking collectives, local(): partial = lax.psum(square_sum / token_count + penalty_part, 'mp')  19.8 us
    psum x1, blocking collectives, local(): loss = lax.psum(partial, 'section')  6.27 us
    psum x1, blocking collectives, local(): lax.psum(layer_norm.astype(jnp.bfloat16), 'section').astype(jnp.float32)  5.77 us
    dot_general x1, matrix products, local(): lax.dot_general(latents, lax.all_gather(grad_rec_t, 'mp', axis=0, tiled=T...  5.49 us
  transfers between devices with their start and end apart: 2, of which 2 were waited for; matrix products, arithmetic and copies ran while one was open for 2% of the time, Pallas kernels for 0%

profile of v1, /device:TPU:0, one launch (start us, length us, event | category | flops | bytes accessed | tf_op | source)
XLA Modules:
  0.0 217.6 jit_solution(13479778094177012924)
XLA Ops:
  7.2 0.0 copy-start
  7.2 0.0 copy-start.2
  7.2 0.0 all-reduce.2.cloned.1.call-start
  7.2 33.2 %all-gather = bf16[1,64,4096]{2,1,0:T(8,128)(2,1)S(1)} all-gather(bf16[1,8,4096]{2,1,0:T(8,128)(2,1)} %param.5), channel_id=2, replica_groups=mesh['section'=4,'mp'=8] {'mp'}, dimensions={1}, use_global_device_ids=true | all-gather | bytes 589824 | tf_op jit(solution)/shard_map/all_gather | solution.py:10
  40.5 3.7 %fusion.7 = bf16[64,512]{1,0:T(8,128)(2,1)} fusion(bf16[1,4096,512]{2,1,0:T(8,128)(2,1)} %param.6, bf16[1,64,4096]{2,1,0:T(8,128)(2,1)S(1)} %all-gather), kind=kOutput, calls=%fused_computation.10 | convolution fusion | flops 268468224 | bytes 4784128 | tf_op jit(solution)/shard_map/dot_general | solution.py:12
  44.1 0.0 all-reduce.2.cloned.1.call-update
  44.2 0.0 reduce-scatter.2.cloned.1.call-start
  44.2 32.7 %all-reduce.2.cloned.1.call-done = bf16[64,512]{1,0:T(8,128)(2,1)} async-done(((bf16[64,512]{1,0:T(8,128)(2,1)}), bf16[64,512]{1,0:T(8,128)(2,1)}) %all-reduce.2.cloned.1.call-update) | async-done | bytes 65552 | tf_op jit(solution)/shard_map/psum | solution.py:16
  76.9 0.0 copy-done.2
  76.9 0.0 copy-start.1
  76.9 4.1 %convolution_bitcast_fusion = f32[4096,64]{0,1:T(8,128)} fusion(bf16[512,1,4096]{2,0,1:T(8,128)(2,1)} %param.8, bf16[64,512]{1,0:T(8,128)(2,1)} %all-reduce.2.cloned.1.call-done, f32[512]{0:T(512)S(1)} %copy-done.2), kind=kOutput, calls=%fused_computation.6 | convolution fusion | flops 268566528 | bytes 5310464 | tf_op jit(solution)/shard_map/dot_general | solution.py:28
  81.0 0.0 reduce-scatter.2.cloned.1.call-update
  81.1 3.1 %fusion = f32[512]{0:T(512)S(1)} fusion(bf16[512,1,4096]{2,0,1:T(8,128)(2,1)} %param.8), kind=kLoop, calls=%fused_computation.2 | loop fusion | flops 6290944 | bytes 4196352 | tf_op jit(solution)/shard_map/reduce_sum | solution.py:14
  84.1 5.8 %psum.29 = bf16[512]{0:T(512)(128)(2,1)S(1)} all-reduce(bf16[512]{0:T(512)(128)(2,1)S(1)} %sqrt_convert_fusion), channel_id=1, replica_groups=mesh['section'=4,'mp'=8] {'section'}, use_global_device_ids=true, to_apply=%region_4.0 | all-reduce | flops 512 | bytes 2048 | tf_op jit(solution)/shard_map/psum | solution.py:17
  89.9 0.0 copy-done
  89.9 0.0 copy-done.1
  89.9 0.6 convert_reduce_fusion
  91.2 54.2 %reduce-scatter.2.cloned.1.call-done = f32[512,64]{0,1:T(8,128)} async-done(((f32[4096,64]{0,1:T(8,128)}), f32[512,64]{0,1:T(8,128)}) %reduce-scatter.2.cloned.1.call-update) | async-done | bytes 131088 | tf_op jit(solution)/shard_map/reduce_scatter | solution.py:27
  145.5 1.5 multiply_reduce_fusion.1
  147.7 19.8 %psum.30 = f32[]{:T(128)} all-reduce(f32[]{:T(128)S(6)} %add.56), channel_id=1, replica_groups=mesh['section'=4,'mp'=8] {'mp'}, use_global_device_ids=true, to_apply=%region_6.7 | all-reduce | flops 1 | bytes 8 | tf_op jit(solution)/shard_map/psum | solution.py:51
  167.5 6.3 %psum.31 = f32[]{:T(128)} all-reduce(f32[]{:T(128)} %psum.30), channel_id=1, replica_groups=mesh['section'=4,'mp'=8] {'section'}, use_global_device_ids=true, to_apply=%region_7.8 | all-reduce | flops 1 | bytes 8 | tf_op jit(solution)/shard_map/psum | solution.py:52
  173.8 31.5 %all_gather.7 = bf16[4096,64]{0,1:T(8,128)(2,1)S(1)} all-gather(bf16[512,64]{0,1:T(8,128)(2,1)S(1)} %get-tuple-element.7), channel_id=1, replica_groups=mesh['section'=4,'mp'=8] {'mp'}, dimensions={0}, use_global_device_ids=true | all-gather | bytes 589824 | tf_op jit(solution)/shard_map/all_gather | solution.py:44
  205.3 5.5 %fusion.3 = bf16[512,1,4096]{2,0,1:T(8,128)(2,1)} fusion(bf16[4096,64]{0,1:T(8,128)(2,1)S(1)} %all_gather.7, bf16[512,1,4096]{2,0,1:T(8,128)(2,1)} %param.8, f32[512]{0:T(512)S(1)} %rsqrt_multiply_fusion, bf16[64,512]{1,0:T(8,128)(2,1)S(1)} %copy-done.1, f32[512]{0:T(512)S(1)} %copy-done.2), kind=kOutput, calls=%fused_computation.5 | convolution fusion | flops 276955136 | bytes 8982528 | tf_op jit(solution)/shard_map/dot_general | solution.py:42
  (4 shorter events, 0.0 us)
Async XLA Ops:
  7.2 82.8 %copy-start = (f32[1,4096]{1,0:T(1,128)S(1)}, f32[1,4096]{1,0:T(1,128)}, u32[]{:S(2)}) copy-start(f32[1,4096]{1,0:T(1,128)} %param.9) | copy-start | bytes 49156
  7.2 69.8 %copy-start.2 = (f32[512]{0:T(512)S(1)}, f32[512]{0:T(512)}, u32[]{:S(2)}) copy-start(f32[512]{0:T(512)} %param.7) | copy-start | bytes 6148
  7.2 69.8 %all-reduce.2.cloned.1.call-start = ((), (), s32[]{:S(2)}) async-start(), calls=%async_computation.1 | async-start | bytes 131072 | tf_op jit(solution)/shard_map/psum | solution.py:16
  44.2 101.3 %reduce-scatter.2.cloned.1.call-start = ((), (), s32[]{:S(2)}) async-start(), calls=%async_computation.2 | async-start | bytes 1179648 | tf_op jit(solution)/shard_map/reduce_scatter | solution.py:27
  76.9 13.0 %copy-start.1 = (bf16[64,512]{1,0:T(8,128)(2,1)S(1)}, bf16[64,512]{1,0:T(8,128)(2,1)}, u32[]{:S(2)}) copy-start(bf16[64,512]{1,0:T(8,128)(2,1)} %all-reduce.2.cloned.1.call-done) | copy-start | bytes 196612
Sparse Core Ops, SparseCore 0:
  44.3 32.6 all-reduce.1
  81.2 64.2 reduce-scatter.1

commit v2 on v0

--- a/solution.py
+++ b/solution.py
@@ -4,6 +4,12 @@
 from jax.sharding import PartitionSpec as P
 
 penalty_weight = 2.0
+
+
+def add_all(shard, name):
+    pieces = lax.all_gather(shard, name, axis=0, tiled=False)
+    acc = pieces.sum(axis=0)
+    return acc
 
 
 def local(activations, enc_weight, enc_bias, dec_weight, dec_bias):
@@ -48,7 +54,7 @@
     grad_dec = (grad_sum + coef[:, None] * w_dec.astype(jnp.float32)).astype(jnp.bfloat16)[
         :, None, :
     ]
-    loss = lax.psum(square_sum / token_count + penalty_part, ("section", "mp"))
+    loss = add_all(square_sum / token_count + penalty_part, ("section", "mp"))
     return (loss, grad_dec, grad_bias)
 
 

time: 231 us -> 232 us (level)
    unnamed x0 -> x1, blocking collectives: none -> 39.8 us
    psum x1 -> x0, blocking collectives: 39.8 us -> none  [local(): loss = lax.psum(square_sum / token_count + penalty_part, ('section', 'mp'))]
where the time goes in v2:
time: 232 us
  blocking collectives  110 us (47%)
  waiting for transfers between devices  87 us (38%)
  between operations  15.4 us (7%)
  matrix products  13.2 us (6%)
  other arithmetic  5.89 us (3%)
    reduce_scatter x1, waiting for transfers between devices, local(): lax.psum_scatter(lax.dot_general(w_dec, latents, (((0,), (1,)), ((), ()))...  54.2 us
    unnamed x1, blocking collectives  39.8 us
    all_gather x1, blocking collectives, local(): all_rows = lax.all_gather(activations[0], 'mp', axis=0, tiled=True)  33.2 us
    psum x1, waiting for transfers between devices, local(): lax.psum(partial_value.astype(jnp.bfloat16), 'section').astype(jnp.float32)  32.7 us
    all_gather x1, blocking collectives, local(): lax.all_gather(grad_rec_t, 'mp', axis=0, tiled=True)  31.2 us
    psum x1, blocking collectives, local(): lax.psum(layer_norm.astype(jnp.bfloat16), 'section').astype(jnp.float32)  5.77 us
    dot_general x1, matrix products, local(): lax.dot_general(latents, lax.all_gather(grad_rec_t, 'mp', axis=0, tiled=T...  5.49 us
  transfers between devices with their start and end apart: 2, of which 2 were waited for; matrix products, arithmetic and copies ran while one was open for 2% of the time, Pallas kernels for 0%

profile of v2, /device:TPU:0, one launch (start us, length us, event | category | flops | bytes accessed | tf_op | source)
XLA Modules:
  0.0 231.8 jit_solution(10686152047950123566)
XLA Ops:
  7.2 0.0 copy-start
  7.2 0.0 copy-start.2
  7.2 0.0 all-reduce.3.cloned.1.call-start
  7.2 33.2 %all-gather = bf16[1,64,4096]{2,1,0:T(8,128)(2,1)S(1)} all-gather(bf16[1,8,4096]{2,1,0:T(8,128)(2,1)} %param.5), channel_id=2, replica_groups=mesh['section'=4,'mp'=8] {'mp'}, dimensions={1}, use_global_device_ids=true | all-gather | bytes 589824 | tf_op jit(solution)/shard_map/all_gather | solution.py:16
  40.5 3.7 %fusion.7 = bf16[64,512]{1,0:T(8,128)(2,1)} fusion(bf16[1,4096,512]{2,1,0:T(8,128)(2,1)} %param.6, bf16[1,64,4096]{2,1,0:T(8,128)(2,1)S(1)} %all-gather), kind=kOutput, calls=%fused_computation.10 | convolution fusion | flops 268468224 | bytes 4784128 | tf_op jit(solution)/shard_map/dot_general | solution.py:18
  44.1 0.0 all-reduce.3.cloned.1.call-update
  44.2 0.0 reduce-scatter.2.cloned.1.call-start
  44.2 32.7 %all-reduce.3.cloned.1.call-done = bf16[64,512]{1,0:T(8,128)(2,1)} async-done(((bf16[64,512]{1,0:T(8,128)(2,1)}), bf16[64,512]{1,0:T(8,128)(2,1)}) %all-reduce.3.cloned.1.call-update) | async-done | bytes 65552 | tf_op jit(solution)/shard_map/psum | solution.py:22
  76.9 0.0 copy-done.2
  76.9 0.0 copy-start.1
  76.9 4.1 %convolution_bitcast_fusion = f32[4096,64]{0,1:T(8,128)} fusion(bf16[512,1,4096]{2,0,1:T(8,128)(2,1)} %param.8, bf16[64,512]{1,0:T(8,128)(2,1)} %all-reduce.3.cloned.1.call-done, f32[512]{0:T(512)S(1)} %copy-done.2), kind=kOutput, calls=%fused_computation.6 | convolution fusion | flops 268566528 | bytes 5310464 | tf_op jit(solution)/shard_map/dot_general | solution.py:34
  81.0 0.0 reduce-scatter.2.cloned.1.call-update
  81.1 3.1 %fusion = f32[512]{0:T(512)S(1)} fusion(bf16[512,1,4096]{2,0,1:T(8,128)(2,1)} %param.8), kind=kLoop, calls=%fused_computation.2 | loop fusion | flops 6290944 | bytes 4196352 | tf_op jit(solution)/shard_map/reduce_sum | solution.py:20
  84.1 5.8 %psum.15 = bf16[512]{0:T(512)(128)(2,1)S(1)} all-reduce(bf16[512]{0:T(512)(128)(2,1)S(1)} %sqrt_convert_fusion), channel_id=1, replica_groups=mesh['section'=4,'mp'=8] {'section'}, use_global_device_ids=true, to_apply=%region_4.0 | all-reduce | flops 512 | bytes 2048 | tf_op jit(solution)/shard_map/psum | solution.py:23
  89.9 0.0 copy-done
  89.9 0.0 copy-done.1
  89.9 0.6 convert_reduce_fusion
  91.2 54.2 %reduce-scatter.2.cloned.1.call-done = f32[512,64]{0,1:T(8,128)} async-done(((f32[4096,64]{0,1:T(8,128)}), f32[512,64]{0,1:T(8,128)}) %reduce-scatter.2.cloned.1.call-update) | async-done | bytes 131088 | tf_op jit(solution)/shard_map/reduce_scatter | solution.py:33
  145.5 1.5 multiply_reduce_fusion.1
  147.7 0.1 dynamic-update-slice
  147.8 39.8 %all-reduce = f32[32]{0:T(128)S(1)} all-reduce(f32[32]{0:T(128)S(1)} %dynamic-update-slice), channel_id=1, replica_groups=mesh['section'=4,'mp'=8] {'section','mp'}, use_global_device_ids=true, to_apply=%add | all-reduce | flops 32 | bytes 256
  187.6 0.6 reduce_sum.57
  188.2 31.2 %all_gather.15 = bf16[4096,64]{0,1:T(8,128)(2,1)S(1)} all-gather(bf16[512,64]{0,1:T(8,128)(2,1)S(1)} %get-tuple-element.7), channel_id=1, replica_groups=mesh['section'=4,'mp'=8] {'mp'}, dimensions={0}, use_global_device_ids=true | all-gather | bytes 589824 | tf_op jit(solution)/shard_map/all_gather | solution.py:50
  219.4 5.5 %fusion.3 = bf16[512,1,4096]{2,0,1:T(8,128)(2,1)} fusion(bf16[4096,64]{0,1:T(8,128)(2,1)S(1)} %all_gather.15, bf16[512,1,4096]{2,0,1:T(8,128)(2,1)} %param.8, f32[512]{0:T(512)S(1)} %rsqrt_multiply_fusion, bf16[64,512]{1,0:T(8,128)(2,1)S(1)} %copy-done.1, f32[512]{0:T(512)S(1)} %copy-done.2), kind=kOutput, calls=%fused_computation.5 | convolution fusion | flops 276955136 | bytes 8982528 | tf_op jit(solution)/shard_map/dot_general | solution.py:48
  (5 shorter events, 0.0 us)
Async XLA Ops:
  7.2 82.8 %copy-start = (f32[1,4096]{1,0:T(1,128)S(1)}, f32[1,4096]{1,0:T(1,128)}, u32[]{:S(2)}) copy-start(f32[1,4096]{1,0:T(1,128)} %param.9) | copy-start | bytes 49156
  7.2 69.8 %copy-start.2 = (f32[512]{0:T(512)S(1)}, f32[512]{0:T(512)}, u32[]{:S(2)}) copy-start(f32[512]{0:T(512)} %param.7) | copy-start | bytes 6148
  7.2 69.8 %all-reduce.3.cloned.1.call-start = ((), (), s32[]{:S(2)}) async-start(), calls=%async_computation.1 | async-start | bytes 131072 | tf_op jit(solution)/shard_map/psum | solution.py:22
  44.2 101.3 %reduce-scatter.2.cloned.1.call-start = ((), (), s32[]{:S(2)}) async-start(), calls=%async_computation.2 | async-start | bytes 1179648 | tf_op jit(solution)/shard_map/reduce_scatter | solution.py:33
  76.9 13.0 %copy-start.1 = (bf16[64,512]{1,0:T(8,128)(2,1)S(1)}, bf16[64,512]{1,0:T(8,128)(2,1)}, u32[]{:S(2)}) copy-start(bf16[64,512]{1,0:T(8,128)(2,1)} %all-reduce.3.cloned.1.call-done) | copy-start | bytes 196612
Sparse Core Ops, SparseCore 0:
  44.3 32.6 all-reduce.2
  81.2 64.2 reduce-scatter.1
